TPU v7x, 32 devices: a whole 2x2x4 slice. The times are simulated.
32 devices in a mesh: row: 4 (over x, core), col: 4 (over z), vir: 2 (over y).
Axes of the slice: x: 2, y: 2, z: 4, core: 2. Of those that a mesh axis runs over, the one named last changes fastest.
Arguments:
- amplitudes: float32 [80, 4, 4, 3, 128, 128], P('vir', 'row', 'col'), may hold values from -6 to 6
- integrals: float32 [80, 4, 4, 3, 128, 128], P('vir', 'row', 'col'), may hold values from -6 to 6
- cycle_terms: float32 [80, 4, 4, 3, 128, 128], P('vir', 'row', 'col'), may hold values from -0.15625 to 0.15625
- ladder_factors: float32 [80, 8, 128, 128], P('vir'), may hold values from -0.375 to 0.375
- live: int32 [80, 4, 4, 3], P('vir', 'row', 'col'), may hold values 0 or 1
Outputs:
- residual: float32 [80, 4, 4, 3, 128, 128], P('vir', 'row', 'col')
All inputs are finite; a program needn't handle non-finite values. No bound on the sum of `live` on one device may be relied on, other than what follows from the above.
Results may differ from a plain program's by a relative error of at most 0.0001.
Values sent between devices are 32-bit elements; how exact they have to be, the bound alone decides.
No kernel may reach another device: no remote copies, remote signals or barrier semaphores. Data moves between devices by JAX's collectives and lax.ppermute only.
A program may use at most 448 MiB of HBM per device.

v0:
```python
import jax
import jax.numpy as jnp
from jax import lax
from jax.sharding import PartitionSpec as P

NT = 80


def extended(block, sides, width):
    for axis, dim in sides:
        count = lax.axis_size(axis)
        forward = [(i, i + 1) for i in range(count - 1)]
        backward = [(target, source) for source, target in forward]
        low = lax.ppermute(
            lax.slice_in_dim(block, block.shape[dim] - width, None, axis=dim), axis, forward
        )
        high = lax.ppermute(lax.slice_in_dim(block, 0, width, axis=dim), axis, backward)
        block = jnp.concatenate([low, block, high], axis=dim)
    return block


def per_device(amplitudes, integrals, cycle_terms, ladder_factors, live):
    local_tiles = amplitudes.shape[0]
    occupied = amplitudes.shape[1]
    band_slots = amplitudes.shape[3]
    tile_size = amplitudes.shape[4]
    factor_count = ladder_factors.shape[1]
    half_band = band_slots // 2
    slot_index = jnp.arange(band_slots)
    global_rows = lax.axis_index("vir") * local_tiles + jnp.arange(local_tiles)
    col_tile = global_rows[:, None] + slot_index[None, :] - half_band
    inside = (col_tile >= 0) & (col_tile < NT)
    keep = ((live == 1) | (slot_index == half_band)[None, None, None, :]) & inside[:, None, None, :]
    keep_float = keep.astype(jnp.float32)[..., None, None]
    amps = amplitudes * keep_float
    pair_tiles = occupied * occupied * band_slots
    joined = jnp.concatenate(
        [cycle_terms.reshape(local_tiles, pair_tiles, tile_size, tile_size), ladder_factors], axis=1
    )
    widened = extended(joined, (("vir", 0),), half_band)
    cycle_ext = widened[:, :pair_tiles].reshape(
        local_tiles + 2 * half_band, occupied, occupied, band_slots, tile_size, tile_size
    )
    factors = widened[:, pair_tiles:]
    cycle_all = lax.all_gather(cycle_ext, "row", axis=1, tiled=True)
    centre = factors[half_band : half_band + local_tiles]
    ladder = jnp.zeros(amplitudes.shape, jnp.float32)
    for term_index in range(factor_count):
        inner = jnp.einsum(
            "axy,aijsyz->aijsxz", centre[:, term_index], amps, precision=lax.Precision.HIGHEST
        )
        parts = []
        for out_slot in range(band_slots):
            right_side = factors[out_slot : out_slot + local_tiles, term_index]
            parts.append(
                jnp.einsum(
                    "aijxz,awz->aijxw",
                    inner[:, :, :, out_slot],
                    right_side,
                    precision=lax.Precision.HIGHEST,
                )
            )
        ladder = ladder + jnp.stack(parts, axis=3)
    piece = lax.all_gather(amps, "col", axis=2, tiled=True)
    slot_sums = []
    for out_slot in range(band_slots):
        summed = jnp.zeros((local_tiles, occupied, occupied, tile_size, tile_size), jnp.float32)
        for in_slot in range(band_slots):
            mid_slot = out_slot - in_slot + half_band
            if 0 <= mid_slot < band_slots:
                cycle_rows = cycle_all[in_slot : in_slot + local_tiles, :, :, mid_slot]
                summed = summed + jnp.einsum(
                    "aiktu,akjuv->aijtv",
                    piece[:, :, :, in_slot],
                    cycle_rows,
                    precision=lax.Precision.HIGHEST,
                )
        slot_sums.append(summed)
    cycle = jnp.stack(slot_sums, axis=3)
    return keep_float * (integrals + ladder + cycle)


def solution(mesh):
    in_specs = (
        P("vir", "row", "col", None, None, None),
        P("vir", "row", "col", None, None, None),
        P("vir", "row", "col", None, None, None),
        P("vir", None, None, None),
        P("vir", "row", "col", None),
    )
    out_specs = P("vir", "row", "col", None, None, None)
    return jax.shard_map(
        per_device, mesh=mesh, in_specs=in_specs, out_specs=out_specs, check_vma=False
    )
```

profile of v0, /device:TPU:0, one launch (start us, length us, event | category | flops | bytes accessed | tf_op | source)
XLA Modules:
  0.0 918.6 jit_solution(8032832479250462117)
XLA Ops:
  6.5 0.8 and_convert_fusion
  7.3 3.8 copy_multiply_fusion
  11.1 4.1 copy.174
  15.2 0.0 all-gather.4.cloned.1.call-update
  15.3 0.0 all-gather.6.cloned.1.call-start
  15.3 3.8 copy.435
  19.1 0.0 copy-start
  19.1 2.1 pad_maximum_fusion.10
  21.2 4.9 collective-permute-start
  26.1 1.3 collective-permute-start.1
  27.4 14.0 %collective-permute-done = f32[1,11,128,128]{3,2,0,1:T(8,128)S(1)} collective-permute-done((f32[1,11,128,128]{3,2,0,1:T(8,128)S(1)}, f32[1,11,128,128]{3,2,0,1:T(8,128)S(1)}, u32[]{:S(2)}, u32[]{:S(2)}) %collective-permute-start) | collective-permute-done | bytes 720928 | tf_op jit(solution)/shard_map/ppermute | solution.py:14
  41.5 4.2 collective-permute-done.1
  45.6 4.2 pad_maximum_fusion
  49.9 0.0 all-gather.6.cloned.1.call-update
  49.9 0.0 slice-start.2
  49.9 0.0 slice-start.3
  49.9 0.0 slice-start.4
  49.9 17.9 %fusion.32 = f32[40,1,1,3,128,128]{4,5,3,0,2,1:T(8,128)S(1)} fusion(f32[40,3]{0,1:T(4,128)S(1)} %bitcast.514, f32[40,1,1,3,128,128]{5,4,3,2,1,0:T(8,128)} %param.5, f32[40,8,128,128]{3,2,1,0:T(8,128)} %param.8), kind=kOutput, calls=%fused_computation.48 | convolution fusion | flops 3021864960 | bytes 18350560 | tf_op jit(solution)/shard_map/axy,aijsyz->aijsxz/dot_general | solution.py:49
  67.8 3.2 copy-done.2
  71.0 8.0 fusion.178
  79.1 18.1 %fusion.35 = f32[40,1,1,3,128,128]{4,5,3,0,2,1:T(8,128)} fusion(f32[40,3]{0,1:T(4,128)S(1)} %bitcast.515, f32[40,1,1,3,128,128]{5,4,3,2,1,0:T(8,128)} %param.5, f32[40,8,128,128]{3,2,1,0:T(8,128)} %param.8), kind=kOutput, calls=%fused_computation.49 | convolution fusion | flops 3021864960 | bytes 18350560 | tf_op jit(solution)/shard_map/axy,aijsyz->aijsxz/dot_general | solution.py:49
  97.2 7.6 fusion.183
  104.9 15.8 %fusion.38 = f32[40,1,1,3,128,128]{4,5,3,0,2,1:T(8,128)} fusion(f32[40,3]{0,1:T(4,128)S(1)} %bitcast.516, f32[40,1,1,3,128,128]{5,4,3,2,1,0:T(8,128)S(1)} %bitcast.501, f32[40,8,128,128]{3,2,1,0:T(8,128)S(1)} %bitcast.499), kind=kOutput, calls=%fused_computation.50 | convolution fusion | flops 3021864960 | bytes 18352128 | tf_op jit(solution)/shard_map/axy,aijsyz->aijsxz/dot_general | solution.py:49
  120.7 7.7 fusion.188
  128.3 15.5 %fusion.41 = f32[40,1,1,3,128,128]{4,5,3,0,2,1:T(8,128)} fusion(f32[40,3]{0,1:T(4,128)S(1)} %bitcast.517, f32[40,1,1,3,128,128]{5,4,3,2,1,0:T(8,128)S(1)} %bitcast.501, f32[40,8,128,128]{3,2,1,0:T(8,128)S(1)} %bitcast.499), kind=kOutput, calls=%fused_computation.51 | convolution fusion | flops 3021864960 | bytes 18352128 | tf_op jit(solution)/shard_map/axy,aijsyz->aijsxz/dot_general | solution.py:49
  143.9 7.7 fusion.193
  151.6 15.6 %fusion.44 = f32[40,1,1,3,128,128]{4,5,3,0,2,1:T(8,128)} fusion(f32[40,3]{0,1:T(4,128)S(1)} %bitcast.518, f32[40,1,1,3,128,128]{5,4,3,2,1,0:T(8,128)S(1)} %bitcast.501, f32[40,8,128,128]{3,2,1,0:T(8,128)S(1)} %bitcast.499), kind=kOutput, calls=%fused_computation.52 | convolution fusion | flops 3021864960 | bytes 18352128 | tf_op jit(solution)/shard_map/axy,aijsyz->aijsxz/dot_general | solution.py:49
  167.2 7.7 fusion.198
  174.9 15.9 %fusion.47 = f32[40,1,1,3,128,128]{4,5,3,0,2,1:T(8,128)} fusion(f32[40,3]{0,1:T(4,128)S(1)} %bitcast.519, f32[40,1,1,3,128,128]{5,4,3,2,1,0:T(8,128)S(1)} %bitcast.501, f32[40,8,128,128]{3,2,1,0:T(8,128)S(1)} %bitcast.499), kind=kOutput, calls=%fused_computation.53 | convolution fusion | flops 3021864960 | bytes 18352128 | tf_op jit(solution)/shard_map/axy,aijsyz->aijsxz/dot_general | solution.py:49
  190.7 7.7 fusion.203
  198.5 15.6 %fusion.50 = f32[40,1,1,3,128,128]{4,5,3,0,2,1:T(8,128)} fusion(f32[40,3]{0,1:T(4,128)S(1)} %bitcast.520, f32[40,1,1,3,128,128]{5,4,3,2,1,0:T(8,128)S(1)} %bitcast.501, f32[40,8,128,128]{3,2,1,0:T(8,128)S(1)} %bitcast.499), kind=kOutput, calls=%fused_computation.54 | convolution fusion | flops 3021864960 | bytes 18352128 | tf_op jit(solution)/shard_map/axy,aijsyz->aijsxz/dot_general | solution.py:49
  214.0 7.9 fusion.208
  221.9 18.1 %fusion.53 = f32[40,1,1,3,128,128]{4,5,3,0,2,1:T(8,128)} fusion(f32[40,3]{0,1:T(4,128)S(1)} %bitcast.521, f32[40,1,1,3,128,128]{5,4,3,2,1,0:T(8,128)} %param.5, f32[40,8,128,128]{3,2,1,0:T(8,128)S(1)} %bitcast.499), kind=kOutput, calls=%fused_computation.55 | convolution fusion | flops 3021864960 | bytes 18352128 | tf_op jit(solution)/shard_map/axy,aijsyz->aijsxz/dot_general | solution.py:49
  240.0 7.6 fusion.215
  247.6 7.7 fusion.182
  255.3 7.8 fusion.186
  263.2 7.7 fusion.187
  270.9 7.7 fusion.191
  278.6 7.9 fusion.192
  286.5 7.7 fusion.196
  294.2 7.7 fusion.197
  301.8 8.1 fusion.201
  309.9 7.6 fusion.202
  317.6 7.8 fusion.206
  325.4 7.7 fusion.207
  333.0 7.7 fusion.211
  340.7 7.9 fusion.212
  348.6 7.7 fusion.218
  356.3 7.7 fusion.177
  363.9 8.1 fusion.181
  372.0 173.2 %all-gather.4.cloned.1.call-done = f32[40,1,4,3,128,128]{5,4,3,1,0,2:T(8,128)} async-done(((f32[40,1,1,3,128,128]{5,4,3,1,0,2:T(8,128)}), f32[40,1,4,3,128,128]{5,4,3,1,0,2:T(8,128)}) %all-gather.4.cloned.1.call-update) | async-done | bytes 31457296 | tf_op jit(solution)/shard_map/all_gather | solution.py:64
  545.2 25.9 %fusion.237 = (f32[40,1,4,1,128,128]{5,4,3,1,0,2:T(8,128)}, f32[40,1,4,1,128,128]{5,4,3,1,0,2:T(8,128)}, f32[40,1,4,1,128,128]{5,4,3,1,0,2:T(8,128)}) fusion(f32[40,1,4,3,128,128]{5,4,3,1,0,2:T(8,128)} %all-gather.4.cloned.1.call-done), kind=kLoop, calls=%fused_computation.267 | loop fusion | bytes 62914560 | tf_op jit(solution)/shard_map/slice | solution.py:74
  571.1 172.4 %all-gather.6.cloned.1.call-done = f32[42,12,128,128]{3,2,0,1:T(8,128)} async-done(((f32[42,3,128,128]{3,2,0,1:T(8,128)}), f32[42,12,128,128]{3,2,0,1:T(8,128)}) %all-gather.6.cloned.1.call-update) | async-done | bytes 33030160 | tf_op jit(solution)/shard_map/all_gather | solution.py:45
  743.6 24.3 %copy.172 = f32[42,12,128,128]{3,2,1,0:T(8,128)} copy(f32[42,12,128,128]{3,2,0,1:T(8,128)} %all-gather.6.cloned.1.call-done) | data formatting | bytes 66060288 | tf_op jit(solution)/shard_map/all_gather | solution.py:45
  767.9 0.3 copy-done.1
  768.2 15.4 %fusion.4 = f32[40,128,128,1]{1,2,3,0:T(8,128)} fusion(f32[42,4,1,3,128,128]{5,4,3,1,0,2:T(8,128)} %bitcast.502, f32[40,1,4,1,128,128]{5,4,3,1,0,2:T(8,128)S(1)} %copy-done.1), kind=kOutput, calls=%fused_computation.9 | convolution fusion | flops 4026531840 | bytes 23592960 | tf_op jit(solution)/shard_map/aiktu,akjuv->aijtv/dot_general | solution.py:72
  783.6 16.2 %fusion.6 = f32[40,128,128,1]{1,2,3,0:T(8,128)S(1)} fusion(f32[42,4,1,3,128,128]{5,4,3,1,0,2:T(8,128)} %bitcast.503, f32[40,1,4,1,128,128]{5,4,3,1,0,2:T(8,128)} %get-tuple-element.5), kind=kOutput, calls=%fused_computation.13 | convolution fusion | flops 4026531840 | bytes 23592960 | tf_op jit(solution)/shard_map/aiktu,akjuv->aijtv/dot_general | solution.py:72
  799.9 15.3 %fusion.3 = f32[40,128,128,1]{1,2,3,0:T(8,128)} fusion(f32[42,4,1,3,128,128]{5,4,3,1,0,2:T(8,128)} %bitcast.504, f32[40,1,4,1,128,128]{5,4,3,1,0,2:T(8,128)S(1)} %bitcast.510), kind=kOutput, calls=%fused_computation.7 | convolution fusion | flops 4026531840 | bytes 23592960 | tf_op jit(solution)/shard_map/aiktu,akjuv->aijtv/dot_general | solution.py:72
  815.2 15.4 %fusion.1 = f32[40,128,128,1]{1,2,3,0:T(8,128)} fusion(f32[42,4,1,3,128,128]{5,4,3,1,0,2:T(8,128)} %bitcast.505, f32[40,1,4,1,128,128]{5,4,3,1,0,2:T(8,128)S(1)} %bitcast.510), kind=kOutput, calls=%fused_computation.3 | convolution fusion | flops 4026531840 | bytes 23592960 | tf_op jit(solution)/shard_map/aiktu,akjuv->aijtv/dot_general | solution.py:72
  830.6 15.6 %fusion.152 = f32[40,1,1,1,128,128]{5,4,0,3,2,1:T(8,128)} fusion(f32[40,128,128,1]{1,2,3,0:T(8,128)S(1)} %fusion.6, f32[40,1,4,1,128,128]{5,4,3,1,0,2:T(8,128)S(1)} %bitcast.510, f32[42,4,1,3,128,128]{5,4,3,1,0,2:T(8,128)} %bitcast.506), kind=kOutput, calls=%fused_computation.196 | convolution fusion | flops 4027187200 | bytes 26214400 | tf_op jit(solution)/shard_map/aiktu,akjuv->aijtv/dot_general | solution.py:72
  846.2 20.5 %fusion.150 = f32[40,1,1,1,128,128]{5,4,0,3,2,1:T(8,128)} fusion(f32[40,128,128,1]{1,2,3,0:T(8,128)} %fusion.1, f32[40,1,4,1,128,128]{5,4,3,1,0,2:T(8,128)} %get-tuple-element.7, f32[42,4,1,3,128,128]{5,4,3,1,0,2:T(8,128)} %bitcast.507), kind=kOutput, calls=%fused_computation.191 | convolution fusion | flops 4027187200 | bytes 26214400 | tf_op jit(solution)/shard_map/aiktu,akjuv->aijtv/dot_general | solution.py:72
  866.7 16.1 %fusion.151 = f32[40,1,1,1,128,128]{5,4,0,3,2,1:T(8,128)} fusion(f32[40,128,128,1]{1,2,3,0:T(8,128)} %fusion.3, f32[40,128,128,1]{1,2,3,0:T(8,128)S(1)} %copy-done.4, f32[40,1,4,1,128,128]{5,4,3,1,0,2:T(8,128)S(1)} %bitcast.512, f32[42,4,1,3,128,128]{5,4,3,1,0,2:T(8,128)} %bitcast.508), kind=kOutput, calls=%fused_computation.193 | convolution fusion | flops 4027842560 | bytes 28835840 | tf_op jit(solution)/shard_map/aiktu,akjuv->aijtv/dot_general | solution.py:72
  882.9 25.0 %fusion.15 = f32[40,1,1,3,128,128]{5,4,0,3,2,1:T(8,128)S(1)} fusion(f32[40,1,1,1,128,128]{5,4,0,3,2,1:T(8,128)} %fusion.181, f32[40,1,1,1,128,128]{5,4,0,3,2,1:T(8,128)} %fusion.178, f32[40,1,1,1,128,128]{5,4,0,3,2,1:T(8,128)} %fusion.177, f32[40,1,1,1,128,128]{5,4,0,3,2,1:T(8,128)} %fusion.186, f32[40,1,1,1,128,128]{5,4,0,3,2,1:T(8,128)} %fusion.183, ...), kind=kLoop, calls=%fused_computation.29 | loop fusion | flops 55050240 | bytes 86508000 | tf_op jit(solution)/shard_map/mul | solution.py:80
  907.8 3.8 copy.191
  (47 shorter events, 0.1 us)
Async XLA Ops:
  6.5 538.7 %all-gather.4.cloned.1.call-start = ((), (), s32[]{:S(2)}) async-start(), calls=%async_computation | async-start | bytes 39321600 | tf_op jit(solution)/shard_map/all_gather | solution.py:64
  7.3 214.6 %copy-start.5 = (f32[40,1,1,3]{0,3,2,1:T(4,128)}, f32[40,1,1,3]{0,3,2,1:T(4,128)S(1)}, u32[]{:S(2)}) copy-start(f32[40,1,1,3]{0,3,2,1:T(4,128)S(1)} %copy.436) | copy-start | bytes 1444
  15.3 728.3 %all-gather.6.cloned.1.call-start = ((), (), s32[]{:S(2)}) async-start(), calls=%async_computation.1 | async-start | bytes 41287680 | tf_op jit(solution)/shard_map/all_gather | solution.py:45
  19.1 26.5 %copy-start = (f32[40,1,1,3,128,128]{5,4,0,3,2,1:T(8,128)}, f32[40,1,1,3,128,128]{5,4,0,3,2,1:T(8,128)S(1)}, u32[]{:S(2)}) copy-start(f32[40,1,1,3,128,128]{5,4,0,3,2,1:T(8,128)S(1)} %copy.435) | copy-start | bytes 23592964
  21.2 20.3 %collective-permute-start = (f32[1,11,128,128]{3,2,0,1:T(8,128)S(1)}, f32[1,11,128,128]{3,2,0,1:T(8,128)S(1)}, u32[]{:S(2)}, u32[]{:S(2)}) collective-permute-start(f32[1,11,128,128]{3,2,0,1:T(8,128)S(1)} %get-tuple-element.8), channel_id=1, source_target_pairs={{0,1},{2,3},{4,5},{6,7},{8,9},{10,11},{12,13},{14,15},{16,17},{18,... | collective-permute-start | bytes 2162696 | tf_op jit(solution)/shard_map/ppermute | solution.py:14
  26.1 19.5 %collective-permute-start.1 = (f32[1,11,128,128]{3,2,0,1:T(8,128)S(1)}, f32[1,11,128,128]{3,2,0,1:T(8,128)S(1)}, u32[]{:S(2)}, u32[]{:S(2)}) collective-permute-start(f32[1,11,128,128]{3,2,0,1:T(8,128)S(1)} %get-tuple-element.9), channel_id=1, source_target_pairs={{1,0},{3,2},{5,4},{7,6},{9,8},{11,10},{13,12},{15,14},{17,16},{19,... | collective-permute-start | bytes 2162696 | tf_op jit(solution)/shard_map/ppermute | solution.py:17
  49.9 47.3 %slice-start.2 = ((s8[20971520]{0:T(1024)(128)(4,1)}), s8[4194304]{0:T(1024)(128)(4,1)S(1)}, s32[]{:S(2)}) async-start(s8[20971520]{0:T(1024)(128)(4,1)} %bitcast.498), calls=%async_computation.4 | async-start | bytes 8388608
  49.9 47.3 %slice-start.3 = ((s8[20971520]{0:T(1024)(128)(4,1)}), s8[4194304]{0:T(1024)(128)(4,1)S(1)}, s32[]{:S(2)}) async-start(s8[20971520]{0:T(1024)(128)(4,1)} %bitcast.498), calls=%async_computation.5 | async-start | bytes 8388608
  49.9 47.3 %slice-start.4 = ((s8[20971520]{0:T(1024)(128)(4,1)}), s8[4194304]{0:T(1024)(128)(4,1)S(1)}, s32[]{:S(2)}) async-start(s8[20971520]{0:T(1024)(128)(4,1)} %bitcast.498), calls=%async_computation.6 | async-start | bytes 8388608
  67.8 3.2 copy-start.2
  71.0 33.9 %slice-start.7 = ((s8[7864320]{0:T(1024)(128)(4,1)}), s8[4194304]{0:T(1024)(128)(4,1)S(1)}, s32[]{:S(2)}) async-start(s8[7864320]{0:T(1024)(128)(4,1)} %bitcast.500), calls=%async_computation.9 | async-start | bytes 8388608
  79.1 18.1 %slice-start.5 = ((s8[20971520]{0:T(1024)(128)(4,1)}), s8[4194304]{0:T(1024)(128)(4,1)S(1)}, s32[]{:S(2)}) async-start(s8[20971520]{0:T(1024)(128)(4,1)} %bitcast.498), calls=%async_computation.7 | async-start | bytes 8388608
  79.1 18.2 %slice-start.6 = ((s8[20971520]{0:T(1024)(128)(4,1)}), s8[4194304]{0:T(1024)(128)(4,1)S(1)}, s32[]{:S(2)}) async-start(s8[20971520]{0:T(1024)(128)(4,1)} %bitcast.498), calls=%async_computation.8 | async-start | bytes 8388608
  79.1 25.8 %slice-start.8 = ((s8[7864320]{0:T(1024)(128)(4,1)}), s8[3670016]{0:T(1024)(128)(4,1)S(1)}, s32[]{:S(2)}) async-start(s8[7864320]{0:T(1024)(128)(4,1)} %bitcast.500), calls=%async_computation.10 | async-start | bytes 7340032
  214.0 33.6 %slice-start = ((s8[7864320]{0:T(1024)(128)(4,1)}), s8[4194304]{0:T(1024)(128)(4,1)S(1)}, s32[]{:S(2)}) async-start(s8[7864320]{0:T(1024)(128)(4,1)} %bitcast.480), calls=%async_computation.2 | async-start | bytes 8388608
  221.9 25.7 %slice-start.1 = ((s8[7864320]{0:T(1024)(128)(4,1)}), s8[3670016]{0:T(1024)(128)(4,1)S(1)}, s32[]{:S(2)}) async-start(s8[7864320]{0:T(1024)(128)(4,1)} %bitcast.480), calls=%async_computation.3 | async-start | bytes 7340032
  743.6 24.7 %copy-start.1 = (f32[40,1,4,1,128,128]{5,4,3,1,0,2:T(8,128)S(1)}, f32[40,1,4,1,128,128]{5,4,3,1,0,2:T(8,128)}, u32[]{:S(2)}) copy-start(f32[40,1,4,1,128,128]{5,4,3,1,0,2:T(8,128)} %get-tuple-element.5) | copy-start | bytes 31457284
  768.2 31.7 %slice-start.9 = ((s8[10485760]{0:T(1024)(128)(4,1)}), s8[4194304]{0:T(1024)(128)(4,1)S(1)}, s32[]{:S(2)}) async-start(s8[10485760]{0:T(1024)(128)(4,1)} %bitcast.509), calls=%async_computation.11 | async-start | bytes 8388608
  768.2 31.7 %slice-start.10 = ((s8[10485760]{0:T(1024)(128)(4,1)}), s8[4194304]{0:T(1024)(128)(4,1)S(1)}, s32[]{:S(2)}) async-start(s8[10485760]{0:T(1024)(128)(4,1)} %bitcast.509), calls=%async_computation.12 | async-start | bytes 8388608
  783.6 16.3 %slice-start.11 = ((s8[10485760]{0:T(1024)(128)(4,1)}), s8[2097152]{0:T(1024)(128)(4,1)S(1)}, s32[]{:S(2)}) async-start(s8[10485760]{0:T(1024)(128)(4,1)} %bitcast.509), calls=%async_computation.13 | async-start | bytes 4194304
  830.6 36.1 %slice-start.12 = ((s8[10485760]{0:T(1024)(128)(4,1)}), s8[2097152]{0:T(1024)(128)(4,1)S(1)}, s32[]{:S(2)}) async-start(s8[10485760]{0:T(1024)(128)(4,1)} %bitcast.511), calls=%async_computation.14 | async-start | bytes 4194304
  830.6 36.1 %slice-start.13 = ((s8[10485760]{0:T(1024)(128)(4,1)}), s8[4194304]{0:T(1024)(128)(4,1)S(1)}, s32[]{:S(2)}) async-start(s8[10485760]{0:T(1024)(128)(4,1)} %bitcast.511), calls=%async_computation.15 | async-start | bytes 8388608
  846.2 20.5 %slice-start.14 = ((s8[10485760]{0:T(1024)(128)(4,1)}), s8[4194304]{0:T(1024)(128)(4,1)S(1)}, s32[]{:S(2)}) async-start(s8[10485760]{0:T(1024)(128)(4,1)} %bitcast.511), calls=%async_computation.16 | async-start | bytes 8388608
  846.2 20.5 %copy-start.4 = (f32[40,128,128,1]{1,2,3,0:T(8,128)S(1)}, f32[40,128,128,1]{1,2,3,0:T(8,128)}, u32[]{:S(2)}) copy-start(f32[40,128,128,1]{1,2,3,0:T(8,128)} %fusion.4) | copy-start | bytes 7864324
  866.7 16.2 %copy-start.3 = (f32[40,1,1,1,128,128]{5,4,0,3,2,1:T(8,128)S(1)}, f32[40,1,1,1,128,128]{5,4,0,3,2,1:T(8,128)}, u32[]{:S(2)}) copy-start(f32[40,1,1,1,128,128]{5,4,0,3,2,1:T(8,128)} %fusion.182) | copy-start | bytes 7864324
  866.7 16.1 %copy-start.6 = (f32[40,1,1,3]{0,3,2,1:T(4,128)S(1)}, f32[40,1,1,3]{0,3,2,1:T(4,128)}, u32[]{:S(2)}) copy-start(f32[40,1,1,3]{0,3,2,1:T(4,128)} %copy-done.5) | copy-start | bytes 1444
Sparse Core Ops, SparseCore 0:
  15.4 529.8 all-gather.3
  546.8 196.6 all-gather.5
where the time goes:
time: 922 us; the launch traced here: 919 us
  matrix products  433 us (47%)
  waiting for transfers between devices  364 us (39%)
  local copies, waits for them, and re-layouts  65.5 us (7%)
  other arithmetic  35.8 us (4%)
  between operations  13.8 us (1%)
    dot_general x24, matrix products, per_device(): jnp.einsum('aijxz,awz->aijxw', inner[:, :, :, out_slot], right_side, prec...  186 us
    all_gather x1, waiting for transfers between devices, per_device(): piece = lax.all_gather(amps, 'col', axis=2, tiled=True)  173 us
    all_gather x1, waiting for transfers between devices, per_device(): cycle_all = lax.all_gather(cycle_ext, 'row', axis=1, tiled=True)  172 us
    dot_general x8, matrix products, per_device(): jnp.einsum('axy,aijsyz->aijsxz', centre[:, term_index], amps, precision=l...  132 us
    dot_general x7, matrix products, per_device(): jnp.einsum('aiktu,akjuv->aijtv', piece[:, :, :, in_slot], cycle_rows, pre...  115 us
    slice x1, local copies, waits for them, and re-layouts, per_device(): piece[:, :, :, in_slot]  25.9 us
    mul x2, other arithmetic, per_device(): return keep_float * (integrals + ladder + cycle)  25.7 us
    all_gather x1, local copies, waits for them, and re-layouts, per_device(): cycle_all = lax.all_gather(cycle_ext, 'row', axis=1, tiled=True)  24.3 us
  transfers between devices with their start and end apart: 4, of which 4 were waited for; matrix products, arithmetic and copies ran while one was open for 39% of the time, Pallas kernels for 0%

commit v1 on v0

--- a/solution.py
+++ b/solution.py
@@ -42,7 +42,12 @@
         local_tiles + 2 * half_band, occupied, occupied, band_slots, tile_size, tile_size
     )
     factors = widened[:, pair_tiles:]
-    cycle_all = lax.all_gather(cycle_ext, "row", axis=1, tiled=True)
+    ring = [cycle_ext]
+    for hop in range(3):
+        ring.append(lax.ppermute(ring[-1], "row", [(dev, (dev + 1) % 4) for dev in range(4)]))
+    cycle_all = jnp.roll(
+        jnp.concatenate(ring[::-1], axis=1), (lax.axis_index("row") + 1) * ring[0].shape[1], axis=1
+    )
     centre = factors[half_band : half_band + local_tiles]
     ladder = jnp.zeros(amplitudes.shape, jnp.float32)
     for term_index in range(factor_count):

time: 922 us -> 705 us (0.76)
  waiting for transfers between devices: 364 us -> 135 us
    all_gather x1 -> x0, waiting for transfers between devices: 172 us -> none  [per_device(): cycle_all = lax.all_gather(cycle_ext, 'row', axis=1, tiled=True)]
    all_gather x1, waiting for transfers between devices: 173 us -> 25.1 us  [per_device(): piece = lax.all_gather(amps, 'col', axis=2, tiled=True)]
    ppermute x0 -> x3, waiting for transfers between devices: none -> 91.6 us  [per_device(): lax.ppermute(ring[-1], 'row', [(dev, (dev + 1) % 4) for dev in range(4)])]
    unnamed x46 -> x53, local copies, waits for them, and re-layouts: 7.45 us -> 60.3 us
    slice x1 -> x0, local copies, waits for them, and re-layouts: 25.9 us -> none  [per_device(): piece[:, :, :, in_slot]]
    all_gather x1 -> x0, local copies, waits for them, and re-layouts: 24.3 us -> none  [per_device(): cycle_all = lax.all_gather(cycle_ext, 'row', axis=1, tiled=True)]
  transfers between devices with their start and end apart: 4 -> 6, of which waited for: 4 -> 4; matrix products, arithmetic and copies ran while one was open for 39% -> 54% of each run, Pallas kernels for 0% -> 0%
where the time goes in v1:
time: 705 us; the launch traced here: 701 us
  matrix products  442 us (63%)
  waiting for transfers between devices  135 us (19%)
  local copies, waits for them, and re-layouts  72.3 us (10%)
  other arithmetic  29.7 us (4%)
  between operations  13.9 us (2%)
  starting transfers between devices  8.11 us (1%)
    dot_general x24, matrix products, per_device(): jnp.einsum('aijxz,awz->aijxw', inner[:, :, :, out_slot], right_side, prec...  186 us
    dot_general x8, matrix products, per_device(): jnp.einsum('axy,aijsyz->aijsxz', centre[:, term_index], amps, precision=l...  133 us
    dot_general x7, matrix products, per_device(): jnp.einsum('aiktu,akjuv->aijtv', piece[:, :, :, in_slot], cycle_rows, pre...  123 us
    ppermute x3, waiting for transfers between devices, per_device(): lax.ppermute(ring[-1], 'row', [(dev, (dev + 1) % 4) for dev in range(4)])  91.6 us
    unnamed x53, local copies, waits for them, and re-layouts  60.3 us
    all_gather x1, waiting for transfers between devices, per_device(): piece = lax.all_gather(amps, 'col', axis=2, tiled=True)  25.1 us
    mul x2, other arithmetic, per_device(): return keep_float * (integrals + ladder + cycle)  22.6 us
  transfers between devices with their start and end apart: 6, of which 4 were waited for; matrix products, arithmetic and copies ran while one was open for 54% of the time, Pallas kernels for 0%

profile of v1, /device:TPU:0, one launch (start us, length us, event | category | flops | bytes accessed | tf_op | source)
XLA Modules:
  0.0 700.8 jit_solution(4906817975415266654)
XLA Ops:
  6.5 0.8 and_convert_fusion
  7.3 3.8 copy_multiply_fusion
  11.1 4.0 copy.116
  15.2 3.8 copy.368
  19.0 2.1 pad_maximum_fusion.10
  21.1 4.9 collective-permute-start
  26.0 1.3 collective-permute-start.1
  27.3 14.0 %collective-permute-done = f32[1,11,128,128]{3,2,0,1:T(8,128)S(1)} collective-permute-done((f32[1,11,128,128]{3,2,0,1:T(8,128)S(1)}, f32[1,11,128,128]{3,2,0,1:T(8,128)S(1)}, u32[]{:S(2)}, u32[]{:S(2)}) %collective-permute-start) | collective-permute-done | bytes 720928 | tf_op jit(solution)/shard_map/ppermute | solution.py:14
  41.4 4.2 collective-permute-done.1
  45.5 1.2 fusion.7
  46.7 3.2 copy-done.1
  49.9 91.6 %collective-permute-done.2 = f32[42,1,1,3,128,128]{5,4,0,3,2,1:T(8,128)} collective-permute-done((f32[42,1,1,3,128,128]{5,4,0,3,2,1:T(8,128)S(1)}, f32[42,1,1,3,128,128]{5,4,0,3,2,1:T(8,128)}, u32[]{:S(2)}, u32[]{:S(2)}) %collective-permute-start.2) | collective-permute-done | bytes 8257568 | tf_op jit(solution)/shard_map/ppermute | solution.py:47
  141.7 18.1 %fusion.33 = f32[40,1,1,3,128,128]{4,5,3,0,2,1:T(8,128)S(1)} fusion(f32[40,3]{0,1:T(4,128)S(1)} %bitcast.502, f32[40,1,1,3,128,128]{5,4,3,2,1,0:T(8,128)} %param.5, f32[40,8,128,128]{3,2,1,0:T(8,128)} %param.8), kind=kOutput, calls=%fused_computation.49 | convolution fusion | flops 3021864960 | bytes 18350560 | tf_op jit(solution)/shard_map/axy,aijsyz->aijsxz/dot_general | solution.py:54
  159.8 3.1 copy-done.2
  162.9 8.0 %fusion.179 = f32[40,1,1,1,128,128]{5,4,0,3,2,1:T(8,128)} fusion(f32[40,1,1,3,128,128]{4,5,3,0,2,1:T(8,128)S(1)} %fusion.33, f32[40,8,128,128]{3,2,1,0:T(8,128)} %param.8), kind=kOutput, calls=%fused_computation.223 | convolution fusion | flops 1006632960 | bytes 7864320 | tf_op jit(solution)/shard_map/aijxz,awz->aijxw/dot_general | solution.py:61
  170.9 18.1 %fusion.36 = f32[40,1,1,3,128,128]{4,5,3,0,2,1:T(8,128)} fusion(f32[40,3]{0,1:T(4,128)S(1)} %bitcast.503, f32[40,1,1,3,128,128]{5,4,3,2,1,0:T(8,128)} %param.5, f32[40,8,128,128]{3,2,1,0:T(8,128)} %param.8), kind=kOutput, calls=%fused_computation.50 | convolution fusion | flops 3021864960 | bytes 18350560 | tf_op jit(solution)/shard_map/axy,aijsyz->aijsxz/dot_general | solution.py:54
  189.0 7.7 %fusion.184 = f32[40,1,1,1,128,128]{5,4,0,3,2,1:T(8,128)} fusion(f32[40,1,1,3,128,128]{4,5,3,0,2,1:T(8,128)} %fusion.36, f32[40,8,128,128]{3,2,1,0:T(8,128)S(1)} %bitcast.496), kind=kOutput, calls=%fused_computation.226 | convolution fusion | flops 1006632960 | bytes 7864320 | tf_op jit(solution)/shard_map/aijxz,awz->aijxw/dot_general | solution.py:61
  196.7 15.6 %fusion.39 = f32[40,1,1,3,128,128]{4,5,3,0,2,1:T(8,128)} fusion(f32[40,3]{0,1:T(4,128)S(1)} %bitcast.504, f32[40,1,1,3,128,128]{5,4,3,2,1,0:T(8,128)S(1)} %bitcast.498, f32[40,8,128,128]{3,2,1,0:T(8,128)S(1)} %bitcast.496), kind=kOutput, calls=%fused_computation.51 | convolution fusion | flops 3021864960 | bytes 18352128 | tf_op jit(solution)/shard_map/axy,aijsyz->aijsxz/dot_general | solution.py:54
  212.4 7.7 %fusion.189 = f32[40,1,1,1,128,128]{5,4,0,3,2,1:T(8,128)} fusion(f32[40,1,1,3,128,128]{4,5,3,0,2,1:T(8,128)} %fusion.39, f32[40,8,128,128]{3,2,1,0:T(8,128)S(1)} %bitcast.496), kind=kOutput, calls=%fused_computation.229 | convolution fusion | flops 1006632960 | bytes 7864320 | tf_op jit(solution)/shard_map/aijxz,awz->aijxw/dot_general | solution.py:61
  220.1 15.7 %fusion.42 = f32[40,1,1,3,128,128]{4,5,3,0,2,1:T(8,128)} fusion(f32[40,3]{0,1:T(4,128)S(1)} %bitcast.505, f32[40,1,1,3,128,128]{5,4,3,2,1,0:T(8,128)S(1)} %bitcast.498, f32[40,8,128,128]{3,2,1,0:T(8,128)S(1)} %bitcast.496), kind=kOutput, calls=%fused_computation.52 | convolution fusion | flops 3021864960 | bytes 18352128 | tf_op jit(solution)/shard_map/axy,aijsyz->aijsxz/dot_general | solution.py:54
  235.7 7.7 %fusion.194 = f32[40,1,1,1,128,128]{5,4,0,3,2,1:T(8,128)} fusion(f32[40,1,1,3,128,128]{4,5,3,0,2,1:T(8,128)} %fusion.42, f32[40,8,128,128]{3,2,1,0:T(8,128)S(1)} %bitcast.496), kind=kOutput, calls=%fused_computation.232 | convolution fusion | flops 1006632960 | bytes 7864320 | tf_op jit(solution)/shard_map/aijxz,awz->aijxw/dot_general | solution.py:61
  243.4 15.6 %fusion.45 = f32[40,1,1,3,128,128]{4,5,3,0,2,1:T(8,128)} fusion(f32[40,3]{0,1:T(4,128)S(1)} %bitcast.506, f32[40,1,1,3,128,128]{5,4,3,2,1,0:T(8,128)S(1)} %bitcast.498, f32[40,8,128,128]{3,2,1,0:T(8,128)S(1)} %bitcast.496), kind=kOutput, calls=%fused_computation.53 | convolution fusion | flops 3021864960 | bytes 18352128 | tf_op jit(solution)/shard_map/axy,aijsyz->aijsxz/dot_general | solution.py:54
  259.1 15.8 %fusion.48 = f32[40,1,1,3,128,128]{4,5,3,0,2,1:T(8,128)} fusion(f32[40,3]{0,1:T(4,128)S(1)} %bitcast.507, f32[40,1,1,3,128,128]{5,4,3,2,1,0:T(8,128)S(1)} %bitcast.498, f32[40,8,128,128]{3,2,1,0:T(8,128)S(1)} %bitcast.496), kind=kOutput, calls=%fused_computation.54 | convolution fusion | flops 3021864960 | bytes 18352128 | tf_op jit(solution)/shard_map/axy,aijsyz->aijsxz/dot_general | solution.py:54
  274.9 1.7 collective-permute-start.4
  276.6 7.6 %fusion.199 = f32[40,1,1,1,128,128]{5,4,0,3,2,1:T(8,128)} fusion(f32[40,1,1,3,128,128]{4,5,3,0,2,1:T(8,128)} %fusion.45, f32[40,8,128,128]{3,2,1,0:T(8,128)S(1)} %bitcast.496), kind=kOutput, calls=%fused_computation.235 | convolution fusion | flops 1006632960 | bytes 7864320 | tf_op jit(solution)/shard_map/aijxz,awz->aijxw/dot_general | solution.py:61
  284.2 7.6 %fusion.204 = f32[40,1,1,1,128,128]{5,4,0,3,2,1:T(8,128)} fusion(f32[40,1,1,3,128,128]{4,5,3,0,2,1:T(8,128)} %fusion.48, f32[40,8,128,128]{3,2,1,0:T(8,128)S(1)} %bitcast.496), kind=kOutput, calls=%fused_computation.238 | convolution fusion | flops 1006632960 | bytes 7864320 | tf_op jit(solution)/shard_map/aijxz,awz->aijxw/dot_general | solution.py:61
  291.9 15.7 %fusion.51 = f32[40,1,1,3,128,128]{4,5,3,0,2,1:T(8,128)} fusion(f32[40,3]{0,1:T(4,128)S(1)} %bitcast.508, f32[40,1,1,3,128,128]{5,4,3,2,1,0:T(8,128)S(1)} %bitcast.498, f32[40,8,128,128]{3,2,1,0:T(8,128)S(1)} %bitcast.496), kind=kOutput, calls=%fused_computation.55 | convolution fusion | flops 3021864960 | bytes 18352128 | tf_op jit(solution)/shard_map/axy,aijsyz->aijsxz/dot_general | solution.py:54
  307.6 7.8 %fusion.209 = f32[40,1,1,1,128,128]{5,4,0,3,2,1:T(8,128)} fusion(f32[40,1,1,3,128,128]{4,5,3,0,2,1:T(8,128)} %fusion.51, f32[40,8,128,128]{3,2,1,0:T(8,128)S(1)} %bitcast.496), kind=kOutput, calls=%fused_computation.241 | convolution fusion | flops 1006632960 | bytes 7864320 | tf_op jit(solution)/shard_map/aijxz,awz->aijxw/dot_general | solution.py:61
  315.4 18.3 %fusion.54 = f32[40,1,1,3,128,128]{4,5,3,0,2,1:T(8,128)} fusion(f32[40,3]{0,1:T(4,128)S(1)} %bitcast.509, f32[40,1,1,3,128,128]{5,4,3,2,1,0:T(8,128)} %param.5, f32[40,8,128,128]{3,2,1,0:T(8,128)S(1)} %bitcast.496), kind=kOutput, calls=%fused_computation.56 | convolution fusion | flops 3021864960 | bytes 18352128 | tf_op jit(solution)/shard_map/axy,aijsyz->aijsxz/dot_general | solution.py:54
  333.7 7.7 %fusion.216 = f32[40,1,1,1,128,128]{5,4,0,3,2,1:T(8,128)} fusion(f32[40,1,1,3,128,128]{4,5,3,0,2,1:T(8,128)} %fusion.54, f32[40,8,128,128]{3,2,1,0:T(8,128)S(1)} %bitcast.496), kind=kOutput, calls=%fused_computation.244 | convolution fusion | flops 1006632960 | bytes 7864320 | tf_op jit(solution)/shard_map/aijxz,awz->aijxw/dot_general | solution.py:61
  341.4 7.7 %fusion.183 = f32[40,1,1,1,128,128]{5,4,0,3,2,1:T(8,128)} fusion(f32[1,11,128,128]{3,2,0,1:T(8,128)S(1)} %collective-permute-done, f32[40,3,128,128]{3,2,0,1:T(8,128)S(1)} %bitcast.479, f32[40,1,1,3,128,128]{4,5,3,0,2,1:T(8,128)} %fusion.36, f32[40,8,128,128]{3,2,1,0:T(8,128)S(1)} %bitcast.496), kind=kOutput, calls=%fused_computation.225 | convolution fusion | flops 1007943680 | bytes 34799616 | tf_op jit(solution)/shard_map/aijxz,awz->aijxw/dot_general | solution.py:61
  349.1 7.9 %fusion.187 = f32[40,1,1,1,128,128]{5,4,0,3,2,1:T(8,128)} fusion(f32[1,11,128,128]{3,2,0,1:T(8,128)S(1)} %collective-permute-done.1, f32[40,3,128,128]{3,2,0,1:T(8,128)S(1)} %bitcast.480, f32[40,1,1,3,128,128]{4,5,3,0,2,1:T(8,128)} %fusion.36, f32[40,8,128,128]{3,2,1,0:T(8,128)S(1)} %bitcast.496), kind=kOutput, calls=%fused_computation.227 | convolution fusion | flops 1007943680 | bytes 34799616 | tf_op jit(solution)/shard_map/aijxz,awz->aijxw/dot_general | solution.py:61
  357.0 7.6 %fusion.188 = f32[40,1,1,1,128,128]{5,4,0,3,2,1:T(8,128)} fusion(f32[1,11,128,128]{3,2,0,1:T(8,128)S(1)} %collective-permute-done, f32[40,3,128,128]{3,2,0,1:T(8,128)S(1)} %bitcast.481, f32[40,1,1,3,128,128]{4,5,3,0,2,1:T(8,128)} %fusion.39, f32[40,8,128,128]{3,2,1,0:T(8,128)S(1)} %bitcast.496), kind=kOutput, calls=%fused_computation.228 | convolution fusion | flops 1007943680 | bytes 34799616 | tf_op jit(solution)/shard_map/aijxz,awz->aijxw/dot_general | solution.py:61
  364.6 7.7 %fusion.192 = f32[40,1,1,1,128,128]{5,4,0,3,2,1:T(8,128)} fusion(f32[1,11,128,128]{3,2,0,1:T(8,128)S(1)} %collective-permute-done.1, f32[40,3,128,128]{3,2,0,1:T(8,128)S(1)} %bitcast.482, f32[40,1,1,3,128,128]{4,5,3,0,2,1:T(8,128)} %fusion.39, f32[40,8,128,128]{3,2,1,0:T(8,128)S(1)} %bitcast.496), kind=kOutput, calls=%fused_computation.230 | convolution fusion | flops 1007943680 | bytes 34799616 | tf_op jit(solution)/shard_map/aijxz,awz->aijxw/dot_general | solution.py:61
  372.3 8.1 %fusion.193 = f32[40,1,1,1,128,128]{5,4,0,3,2,1:T(8,128)} fusion(f32[1,11,128,128]{3,2,0,1:T(8,128)S(1)} %collective-permute-done, f32[40,3,128,128]{3,2,0,1:T(8,128)S(1)} %bitcast.483, f32[40,1,1,3,128,128]{4,5,3,0,2,1:T(8,128)} %fusion.42, f32[40,8,128,128]{3,2,1,0:T(8,128)S(1)} %bitcast.496), kind=kOutput, calls=%fused_computation.231 | convolution fusion | flops 1007943680 | bytes 34799616 | tf_op jit(solution)/shard_map/aijxz,awz->aijxw/dot_general | solution.py:61
  380.4 7.7 %fusion.197 = f32[40,1,1,1,128,128]{5,4,0,3,2,1:T(8,128)} fusion(f32[1,11,128,128]{3,2,0,1:T(8,128)S(1)} %collective-permute-done.1, f32[40,3,128,128]{3,2,0,1:T(8,128)S(1)} %bitcast.484, f32[40,1,1,3,128,128]{4,5,3,0,2,1:T(8,128)} %fusion.42, f32[40,8,128,128]{3,2,1,0:T(8,128)S(1)} %bitcast.496), kind=kOutput, calls=%fused_computation.233 | convolution fusion | flops 1007943680 | bytes 34799616 | tf_op jit(solution)/shard_map/aijxz,awz->aijxw/dot_general | solution.py:61
  388.1 7.6 %fusion.198 = f32[40,1,1,1,128,128]{5,4,0,3,2,1:T(8,128)} fusion(f32[1,11,128,128]{3,2,0,1:T(8,128)S(1)} %collective-permute-done, f32[40,3,128,128]{3,2,0,1:T(8,128)S(1)} %bitcast.485, f32[40,1,1,3,128,128]{4,5,3,0,2,1:T(8,128)} %fusion.45, f32[40,8,128,128]{3,2,1,0:T(8,128)S(1)} %bitcast.496), kind=kOutput, calls=%fused_computation.234 | convolution fusion | flops 1007943680 | bytes 34799616 | tf_op jit(solution)/shard_map/aijxz,awz->aijxw/dot_general | solution.py:61
  395.7 7.9 %fusion.202 = f32[40,1,1,1,128,128]{5,4,0,3,2,1:T(8,128)} fusion(f32[1,11,128,128]{3,2,0,1:T(8,128)S(1)} %collective-permute-done.1, f32[40,3,128,128]{3,2,0,1:T(8,128)S(1)} %bitcast.486, f32[40,1,1,3,128,128]{4,5,3,0,2,1:T(8,128)} %fusion.45, f32[40,8,128,128]{3,2,1,0:T(8,128)S(1)} %bitcast.496), kind=kOutput, calls=%fused_computation.236 | convolution fusion | flops 1007943680 | bytes 34799616 | tf_op jit(solution)/shard_map/aijxz,awz->aijxw/dot_general | solution.py:61
  403.7 7.7 %fusion.203 = f32[40,1,1,1,128,128]{5,4,0,3,2,1:T(8,128)} fusion(f32[1,11,128,128]{3,2,0,1:T(8,128)S(1)} %collective-permute-done, f32[40,3,128,128]{3,2,0,1:T(8,128)S(1)} %bitcast.487, f32[40,1,1,3,128,128]{4,5,3,0,2,1:T(8,128)} %fusion.48, f32[40,8,128,128]{3,2,1,0:T(8,128)S(1)} %bitcast.496), kind=kOutput, calls=%fused_computation.237 | convolution fusion | flops 1007943680 | bytes 34799616 | tf_op jit(solution)/shard_map/aijxz,awz->aijxw/dot_general | solution.py:61
  411.3 7.9 %fusion.207 = f32[40,1,1,1,128,128]{5,4,0,3,2,1:T(8,128)} fusion(f32[1,11,128,128]{3,2,0,1:T(8,128)S(1)} %collective-permute-done.1, f32[40,3,128,128]{3,2,0,1:T(8,128)S(1)} %bitcast.488, f32[40,1,1,3,128,128]{4,5,3,0,2,1:T(8,128)} %fusion.48, f32[40,8,128,128]{3,2,1,0:T(8,128)S(1)} %bitcast.496), kind=kOutput, calls=%fused_computation.239 | convolution fusion | flops 1007943680 | bytes 34799616 | tf_op jit(solution)/shard_map/aijxz,awz->aijxw/dot_general | solution.py:61
  419.2 7.7 %fusion.208 = f32[40,1,1,1,128,128]{5,4,0,3,2,1:T(8,128)} fusion(f32[1,11,128,128]{3,2,0,1:T(8,128)S(1)} %collective-permute-done, f32[40,3,128,128]{3,2,0,1:T(8,128)S(1)} %bitcast.489, f32[40,1,1,3,128,128]{4,5,3,0,2,1:T(8,128)} %fusion.51, f32[40,8,128,128]{3,2,1,0:T(8,128)S(1)} %bitcast.496), kind=kOutput, calls=%fused_computation.240 | convolution fusion | flops 1007943680 | bytes 34799616 | tf_op jit(solution)/shard_map/aijxz,awz->aijxw/dot_general | solution.py:61
  426.9 7.6 %fusion.212 = f32[40,1,1,1,128,128]{5,4,0,3,2,1:T(8,128)} fusion(f32[1,11,128,128]{3,2,0,1:T(8,128)S(1)} %collective-permute-done.1, f32[40,3,128,128]{3,2,0,1:T(8,128)S(1)} %bitcast.490, f32[40,1,1,3,128,128]{4,5,3,0,2,1:T(8,128)} %fusion.51, f32[40,8,128,128]{3,2,1,0:T(8,128)S(1)} %bitcast.496), kind=kOutput, calls=%fused_computation.242 | convolution fusion | flops 1007943680 | bytes 34799616 | tf_op jit(solution)/shard_map/aijxz,awz->aijxw/dot_general | solution.py:61
  434.5 8.0 %fusion.213 = f32[40,1,1,1,128,128]{5,4,0,3,2,1:T(8,128)} fusion(f32[1,11,128,128]{3,2,0,1:T(8,128)S(1)} %collective-permute-done, f32[40,3,128,128]{3,2,0,1:T(8,128)S(1)} %bitcast.491, f32[40,1,1,3,128,128]{4,5,3,0,2,1:T(8,128)} %fusion.54, f32[40,8,128,128]{3,2,1,0:T(8,128)S(1)} %bitcast.496), kind=kOutput, calls=%fused_computation.243 | convolution fusion | flops 1007943680 | bytes 34799616 | tf_op jit(solution)/shard_map/aijxz,awz->aijxw/dot_general | solution.py:61
  442.6 7.7 %fusion.219 = f32[40,1,1,1,128,128]{5,4,0,3,2,1:T(8,128)} fusion(f32[1,11,128,128]{3,2,0,1:T(8,128)S(1)} %collective-permute-done.1, f32[40,3,128,128]{3,2,0,1:T(8,128)S(1)} %bitcast.492, f32[40,1,1,3,128,128]{4,5,3,0,2,1:T(8,128)} %fusion.54, f32[40,8,128,128]{3,2,1,0:T(8,128)S(1)} %bitcast.496), kind=kOutput, calls=%fused_computation.245 | convolution fusion | flops 1007943680 | bytes 34799616 | tf_op jit(solution)/shard_map/aijxz,awz->aijxw/dot_general | solution.py:61
  450.3 7.6 %fusion.178 = f32[40,1,1,1,128,128]{5,4,0,3,2,1:T(8,128)} fusion(f32[1,11,128,128]{3,2,0,1:T(8,128)S(1)} %collective-permute-done, f32[40,3,128,128]{3,2,0,1:T(8,128)S(1)} %bitcast.493, f32[40,1,1,3,128,128]{4,5,3,0,2,1:T(8,128)} %copy-done.2, f32[40,8,128,128]{3,2,1,0:T(8,128)S(1)} %bitcast.496), kind=kOutput, calls=%fused_computation.222 | convolution fusion | flops 1007943680 | bytes 34799616 | tf_op jit(solution)/shard_map/aijxz,awz->aijxw/dot_general | solution.py:61
  457.9 7.8 %fusion.182 = f32[40,1,1,1,128,128]{5,4,0,3,2,1:T(8,128)} fusion(f32[1,11,128,128]{3,2,0,1:T(8,128)S(1)} %collective-permute-done.1, f32[40,3,128,128]{3,2,0,1:T(8,128)S(1)} %bitcast.494, f32[40,1,1,3,128,128]{4,5,3,0,2,1:T(8,128)} %copy-done.2, f32[40,8,128,128]{3,2,1,0:T(8,128)S(1)} %bitcast.496), kind=kOutput, calls=%fused_computation.224 | convolution fusion | flops 1007943680 | bytes 34799616 | tf_op jit(solution)/shard_map/aijxz,awz->aijxw/dot_general | solution.py:61
  465.7 7.7 %constant_dynamic-update-slice_fusion.7 = f32[42,8,1,3,128,128]{5,4,0,3,2,1:T(8,128)} fusion(f32[42,1,1,3,128,128]{5,4,0,3,2,1:T(8,128)} %collective-permute-done.4), kind=kLoop, calls=%fused_computation.255 | loop fusion | bytes 16515072
  473.4 7.8 %constant_dynamic-update-slice_fusion.6 = f32[42,8,1,3,128,128]{5,4,0,3,2,1:T(8,128)} fusion(f32[42,8,1,3,128,128]{5,4,0,3,2,1:T(8,128)} %constant_dynamic-update-slice_fusion.7, f32[42,1,1,3,128,128]{5,4,0,3,2,1:T(8,128)} %collective-permute-done.3), kind=kLoop, calls=%fused_computation.254 | loop fusion | bytes 16515072
  481.1 7.8 %constant_dynamic-update-slice_fusion.5 = f32[42,8,1,3,128,128]{5,4,0,3,2,1:T(8,128)} fusion(f32[42,8,1,3,128,128]{5,4,0,3,2,1:T(8,128)} %constant_dynamic-update-slice_fusion.6, f32[42,1,1,3,128,128]{5,4,0,3,2,1:T(8,128)} %collective-permute-done.2), kind=kLoop, calls=%fused_computation.253 | loop fusion | bytes 16515072
  488.9 4.2 constant_dynamic-update-slice_fusion.4
  493.1 7.6 %constant_dynamic-update-slice_fusion.3 = f32[42,8,1,3,128,128]{5,4,0,3,2,1:T(8,128)} fusion(f32[42,8,1,3,128,128]{5,4,0,3,2,1:T(8,128)} %constant_dynamic-update-slice_fusion.4, f32[42,1,1,3,128,128]{5,4,0,3,2,1:T(8,128)} %collective-permute-done.4), kind=kLoop, calls=%fused_computation.251 | loop fusion | bytes 16515072
  500.7 7.6 %constant_dynamic-update-slice_fusion.2 = f32[42,8,1,3,128,128]{5,4,0,3,2,1:T(8,128)} fusion(f32[42,8,1,3,128,128]{5,4,0,3,2,1:T(8,128)} %constant_dynamic-update-slice_fusion.3, f32[42,1,1,3,128,128]{5,4,0,3,2,1:T(8,128)} %collective-permute-done.3), kind=kLoop, calls=%fused_computation.250 | loop fusion | bytes 16515072
  508.3 7.6 %constant_dynamic-update-slice_fusion.1 = f32[42,8,1,3,128,128]{5,4,0,3,2,1:T(8,128)} fusion(f32[42,8,1,3,128,128]{5,4,0,3,2,1:T(8,128)} %constant_dynamic-update-slice_fusion.2, f32[42,1,1,3,128,128]{5,4,0,3,2,1:T(8,128)} %collective-permute-done.2), kind=kLoop, calls=%fused_computation.249 | loop fusion | bytes 16515072
  515.8 4.2 constant_dynamic-update-slice_fusion
  520.1 25.1 %all-gather.2.cloned.1.call-done = f32[40,1,4,3,128,128]{5,4,3,1,0,2:T(8,128)} async-done(((f32[40,1,1,3,128,128]{5,4,3,1,0,2:T(8,128)}), f32[40,1,4,3,128,128]{5,4,3,1,0,2:T(8,128)}) %all-gather.2.cloned.1.call-update) | async-done | bytes 31457296 | tf_op jit(solution)/shard_map/all_gather | solution.py:69
  545.2 16.2 %fusion.6 = f32[40,128,128,1]{1,2,0,3:T(8,128)S(1)} fusion(f32[42,8,1,3,128,128]{5,4,0,3,2,1:T(8,128)} %constant_dynamic-update-slice_fusion, s32[]{:T(128)S(6)} %select_n.14, s32[]{:T(128)S(6)} %add.193, f32[40,1,4,3,128,128]{5,4,3,1,0,2:T(8,128)} %all-gather.2.cloned.1.call-done), kind=kOutput, calls=%fused_computation.16 | convolution fusion | flops 4026531840 | bytes 23592968 | tf_op jit(solution)/shard_map/aiktu,akjuv->aijtv/dot_general | solution.py:77
  561.4 17.6 %fusion.3 = f32[40,128,128,1]{1,2,0,3:T(8,128)} fusion(f32[42,8,1,3,128,128]{5,4,0,3,2,1:T(8,128)} %constant_dynamic-update-slice_fusion, s32[]{:T(128)S(6)} %add.193, s32[]{:T(128)S(6)} %select_n.14, f32[40,1,4,3,128,128]{5,4,3,1,0,2:T(8,128)} %all-gather.2.cloned.1.call-done), kind=kOutput, calls=%fused_computation.8 | convolution fusion | flops 4026531840 | bytes 23592968 | tf_op jit(solution)/shard_map/aiktu,akjuv->aijtv/dot_general | solution.py:77
  578.9 17.6 %fusion.4 = f32[40,128,128,1]{1,2,0,3:T(8,128)} fusion(f32[42,8,1,3,128,128]{5,4,0,3,2,1:T(8,128)} %constant_dynamic-update-slice_fusion, s32[]{:T(128)S(6)} %select_n.14, s32[]{:T(128)S(6)} %add.195, f32[40,1,4,3,128,128]{5,4,3,1,0,2:T(8,128)} %all-gather.2.cloned.1.call-done), kind=kOutput, calls=%fused_computation.10 | convolution fusion | flops 4026531840 | bytes 23592968 | tf_op jit(solution)/shard_map/aiktu,akjuv->aijtv/dot_general | solution.py:77
  596.5 16.4 %fusion.1 = f32[40,128,128,1]{1,2,0,3:T(8,128)S(1)} fusion(f32[42,8,1,3,128,128]{5,4,0,3,2,1:T(8,128)} %constant_dynamic-update-slice_fusion, s32[]{:T(128)S(6)} %add.193, s32[]{:T(128)S(6)} %select_n.14, s32[]{:T(128)S(6)} %add.195, f32[40,1,4,3,128,128]{5,4,3,1,0,2:T(8,128)} %all-gather.2.cloned.1.call-done), kind=kOutput, calls=%fused_computation.3 | convolution fusion | flops 4026531840 | bytes 23592972 | tf_op jit(solution)/shard_map/aiktu,akjuv->aijtv/dot_general | solution.py:77
  613.0 17.8 %fusion.153 = f32[40,1,1,1,128,128]{5,4,0,3,2,1:T(8,128)} fusion(f32[40,128,128,1]{1,2,0,3:T(8,128)S(1)} %fusion.6, f32[40,1,4,3,128,128]{5,4,3,1,0,2:T(8,128)} %all-gather.2.cloned.1.call-done, f32[42,8,1,3,128,128]{5,4,0,3,2,1:T(8,128)} %constant_dynamic-update-slice_fusion, s32[]{:T(128)S(6)} %add.193, s32[]{:T(128)S(6)} %select_n.14), kind=kOutput, calls=%fused_computation.197 | convolution fusion | flops 4027187200 | bytes 26214408 | tf_op jit(solution)/shard_map/aiktu,akjuv->aijtv/dot_general | solution.py:77
  630.8 18.0 %fusion.151 = f32[40,1,1,1,128,128]{5,4,0,3,2,1:T(8,128)} fusion(f32[40,128,128,1]{1,2,0,3:T(8,128)S(1)} %fusion.1, f32[40,1,4,3,128,128]{5,4,3,1,0,2:T(8,128)} %all-gather.2.cloned.1.call-done, f32[42,8,1,3,128,128]{5,4,0,3,2,1:T(8,128)} %constant_dynamic-update-slice_fusion, s32[]{:T(128)S(6)} %add.195, s32[]{:T(128)S(6)} %select_n.14, s32[]{:T(128)S(6)} %add.193), kind=kOutput, calls=%fused_computation.192 | convolution fusion | flops 4027187200 | bytes 26214412 | tf_op jit(solution)/shard_map/aiktu,akjuv->aijtv/dot_general | solution.py:77
  648.8 19.2 %fusion.152 = f32[40,1,1,1,128,128]{5,4,0,3,2,1:T(8,128)} fusion(f32[40,128,128,1]{1,2,0,3:T(8,128)S(1)} %copy-done.8, f32[40,128,128,1]{1,2,0,3:T(8,128)} %fusion.4, f32[40,1,4,3,128,128]{5,4,3,1,0,2:T(8,128)} %all-gather.2.cloned.1.call-done, f32[42,8,1,3,128,128]{5,4,0,3,2,1:T(8,128)} %constant_dynamic-update-slice_fusion, s32[]{:T(128)S(6)} %add.195, ...), kind=kOutput, calls=%fused_computation.194 | convolution fusion | flops 4027842560 | bytes 28835848 | tf_op jit(solution)/shard_map/aiktu,akjuv->aijtv/dot_general | solution.py:77
  668.0 21.9 %fusion.16 = f32[40,1,1,3,128,128]{5,4,0,3,2,1:T(8,128)S(1)} fusion(f32[40,1,1,1,128,128]{5,4,0,3,2,1:T(8,128)} %fusion.182, f32[40,1,1,1,128,128]{5,4,0,3,2,1:T(8,128)} %fusion.179, f32[40,1,1,1,128,128]{5,4,0,3,2,1:T(8,128)} %fusion.178, f32[40,1,1,1,128,128]{5,4,0,3,2,1:T(8,128)S(1)} %copy-done.4, f32[40,1,1,1,128,128]{5,4,0,3,2,1:T(8,128)} %fusion.184, ...), kind=kLoop, calls=%fused_computation.30 | loop fusion | flops 55050240 | bytes 86508000 | tf_op jit(solution)/shard_map/mul | solution.py:85
  689.9 3.8 copy.134
  (55 shorter events, 0.3 us)
Async XLA Ops:
  6.5 538.6 %all-gather.2.cloned.1.call-start = ((), (), s32[]{:S(2)}) async-start(), calls=%async_computation | async-start | bytes 39321600 | tf_op jit(solution)/shard_map/all_gather | solution.py:69
  7.3 308.1 %copy-start.9 = (f32[40,1,1,3]{0,3,2,1:T(4,128)}, f32[40,1,1,3]{0,3,2,1:T(4,128)S(1)}, u32[]{:S(2)}) copy-start(f32[40,1,1,3]{0,3,2,1:T(4,128)S(1)} %copy.369) | copy-start | bytes 1444
  19.0 26.5 %copy-start = (f32[40,1,1,3,128,128]{5,4,0,3,2,1:T(8,128)}, f32[40,1,1,3,128,128]{5,4,0,3,2,1:T(8,128)S(1)}, u32[]{:S(2)}) copy-start(f32[40,1,1,3,128,128]{5,4,0,3,2,1:T(8,128)S(1)} %copy.368) | copy-start | bytes 23592964
  21.1 20.3 %collective-permute-start = (f32[1,11,128,128]{3,2,0,1:T(8,128)S(1)}, f32[1,11,128,128]{3,2,0,1:T(8,128)S(1)}, u32[]{:S(2)}, u32[]{:S(2)}) collective-permute-start(f32[1,11,128,128]{3,2,0,1:T(8,128)S(1)} %get-tuple-element.5), channel_id=1, source_target_pairs={{0,1},{2,3},{4,5},{6,7},{8,9},{10,11},{12,13},{14,15},{16,17},{18,... | collective-permute-start | bytes 2162696 | tf_op jit(solution)/shard_map/ppermute | solution.py:14
  26.0 19.5 %collective-permute-start.1 = (f32[1,11,128,128]{3,2,0,1:T(8,128)S(1)}, f32[1,11,128,128]{3,2,0,1:T(8,128)S(1)}, u32[]{:S(2)}, u32[]{:S(2)}) collective-permute-start(f32[1,11,128,128]{3,2,0,1:T(8,128)S(1)} %get-tuple-element.6), channel_id=1, source_target_pairs={{1,0},{3,2},{5,4},{7,6},{9,8},{11,10},{13,12},{15,14},{17,16},{19,... | collective-permute-start | bytes 2162696 | tf_op jit(solution)/shard_map/ppermute | solution.py:17
  46.7 3.2 copy-start.1
  49.9 91.6 %collective-permute-start.2 = (f32[42,1,1,3,128,128]{5,4,0,3,2,1:T(8,128)S(1)}, f32[42,1,1,3,128,128]{5,4,0,3,2,1:T(8,128)}, u32[]{:S(2)}, u32[]{:S(2)}) collective-permute-start(f32[42,1,1,3,128,128]{5,4,0,3,2,1:T(8,128)S(1)} %fusion.7), channel_id=1, source_target_pairs={{0,8},{8,16},{16,24},{24,0},{1,9},{9,17},{17,25},{25,1},{2,10},{10... | collective-permute-start | bytes 24772616 | tf_op jit(solution)/shard_map/ppermute | solution.py:47
  141.5 133.4 %collective-permute-start.3 = (f32[42,1,1,3,128,128]{5,4,0,3,2,1:T(8,128)}, f32[42,1,1,3,128,128]{5,4,0,3,2,1:T(8,128)}, u32[]{:S(2)}, u32[]{:S(2)}) collective-permute-start(f32[42,1,1,3,128,128]{5,4,0,3,2,1:T(8,128)} %collective-permute-done.2), channel_id=1, source_target_pairs={{0,8},{8,16},{16,24},{24,0},{1,9},{9,17},{17,25},{25,1},{2,10},{10... | collective-permute-start | bytes 24772616 | tf_op jit(solution)/shard_map/ppermute | solution.py:47
  141.7 47.3 %slice-start.2 = ((s8[20971520]{0:T(1024)(128)(4,1)}), s8[4194304]{0:T(1024)(128)(4,1)S(1)}, s32[]{:S(2)}) async-start(s8[20971520]{0:T(1024)(128)(4,1)} %bitcast.495), calls=%async_computation.3 | async-start | bytes 8388608
  141.7 47.3 %slice-start.3 = ((s8[20971520]{0:T(1024)(128)(4,1)}), s8[4194304]{0:T(1024)(128)(4,1)S(1)}, s32[]{:S(2)}) async-start(s8[20971520]{0:T(1024)(128)(4,1)} %bitcast.495), calls=%async_computation.4 | async-start | bytes 8388608
  141.7 47.3 %slice-start.4 = ((s8[20971520]{0:T(1024)(128)(4,1)}), s8[4194304]{0:T(1024)(128)(4,1)S(1)}, s32[]{:S(2)}) async-start(s8[20971520]{0:T(1024)(128)(4,1)} %bitcast.495), calls=%async_computation.5 | async-start | bytes 8388608
  159.8 3.1 copy-start.2
  162.9 33.8 %slice-start.7 = ((s8[7864320]{0:T(1024)(128)(4,1)}), s8[4194304]{0:T(1024)(128)(4,1)S(1)}, s32[]{:S(2)}) async-start(s8[7864320]{0:T(1024)(128)(4,1)} %bitcast.497), calls=%async_computation.8 | async-start | bytes 8388608
  170.9 18.1 %slice-start.5 = ((s8[20971520]{0:T(1024)(128)(4,1)}), s8[4194304]{0:T(1024)(128)(4,1)S(1)}, s32[]{:S(2)}) async-start(s8[20971520]{0:T(1024)(128)(4,1)} %bitcast.495), calls=%async_computation.6 | async-start | bytes 8388608
  170.9 18.1 %slice-start.6 = ((s8[20971520]{0:T(1024)(128)(4,1)}), s8[4194304]{0:T(1024)(128)(4,1)S(1)}, s32[]{:S(2)}) async-start(s8[20971520]{0:T(1024)(128)(4,1)} %bitcast.495), calls=%async_computation.7 | async-start | bytes 8388608
  170.9 25.9 %slice-start.8 = ((s8[7864320]{0:T(1024)(128)(4,1)}), s8[3670016]{0:T(1024)(128)(4,1)S(1)}, s32[]{:S(2)}) async-start(s8[7864320]{0:T(1024)(128)(4,1)} %bitcast.497), calls=%async_computation.9 | async-start | bytes 7340032
  274.9 190.8 %collective-permute-start.4 = (f32[42,1,1,3,128,128]{5,4,0,3,2,1:T(8,128)}, f32[42,1,1,3,128,128]{5,4,0,3,2,1:T(8,128)}, u32[]{:S(2)}, u32[]{:S(2)}) collective-permute-start(f32[42,1,1,3,128,128]{5,4,0,3,2,1:T(8,128)} %collective-permute-done.3), channel_id=1, source_target_pairs={{0,8},{8,16},{16,24},{24,0},{1,9},{9,17},{17,25},{25,1},{2,10},{10... | collective-permute-start | bytes 24772616 | tf_op jit(solution)/shard_map/ppermute | solution.py:47
  307.6 33.9 %slice-start = ((s8[7864320]{0:T(1024)(128)(4,1)}), s8[4194304]{0:T(1024)(128)(4,1)S(1)}, s32[]{:S(2)}) async-start(s8[7864320]{0:T(1024)(128)(4,1)} %bitcast.477), calls=%async_computation.1 | async-start | bytes 8388608
  315.4 26.1 %slice-start.1 = ((s8[7864320]{0:T(1024)(128)(4,1)}), s8[3670016]{0:T(1024)(128)(4,1)S(1)}, s32[]{:S(2)}) async-start(s8[7864320]{0:T(1024)(128)(4,1)} %bitcast.477), calls=%async_computation.2 | async-start | bytes 7340032
  473.4 15.5 %slice-start.9 = ((s8[8257536]{0:T(1024)(128)(4,1)}), s8[4194304]{0:T(1024)(128)(4,1)S(1)}, s32[]{:S(2)}) async-start(s8[8257536]{0:T(1024)(128)(4,1)} %bitcast.499), calls=%async_computation.10 | async-start | bytes 8388608
  481.1 7.8 %slice-start.10 = ((s8[8257536]{0:T(1024)(128)(4,1)}), s8[4063232]{0:T(1024)(128)(4,1)S(1)}, s32[]{:S(2)}) async-start(s8[8257536]{0:T(1024)(128)(4,1)} %bitcast.499), calls=%async_computation.11 | async-start | bytes 8126464
  630.8 18.0 %copy-start.8 = (f32[40,128,128,1]{1,2,0,3:T(8,128)S(1)}, f32[40,128,128,1]{1,2,0,3:T(8,128)}, u32[]{:S(2)}) copy-start(f32[40,128,128,1]{1,2,0,3:T(8,128)} %fusion.3) | copy-start | bytes 7864324
  648.7 19.3 %copy-start.3 = (f32[40,1,1,1,128,128]{5,4,0,3,2,1:T(8,128)S(1)}, f32[40,1,1,1,128,128]{5,4,0,3,2,1:T(8,128)}, u32[]{:S(2)}) copy-start(f32[40,1,1,1,128,128]{5,4,0,3,2,1:T(8,128)} %fusion.183) | copy-start | bytes 7864324
  648.7 19.3 %copy-start.4 = (f32[40,1,1,1,128,128]{5,4,0,3,2,1:T(8,128)S(1)}, f32[40,1,1,1,128,128]{5,4,0,3,2,1:T(8,128)}, u32[]{:S(2)}) copy-start(f32[40,1,1,1,128,128]{5,4,0,3,2,1:T(8,128)} %fusion.187) | copy-start | bytes 7864324
  648.7 19.3 %copy-start.5 = (f32[40,1,1,1,128,128]{5,4,0,3,2,1:T(8,128)S(1)}, f32[40,1,1,1,128,128]{5,4,0,3,2,1:T(8,128)}, u32[]{:S(2)}) copy-start(f32[40,1,1,1,128,128]{5,4,0,3,2,1:T(8,128)} %fusion.188) | copy-start | bytes 7864324
  648.7 19.3 %copy-start.6 = (f32[40,1,1,1,128,128]{5,4,0,3,2,1:T(8,128)S(1)}, f32[40,1,1,1,128,128]{5,4,0,3,2,1:T(8,128)}, u32[]{:S(2)}) copy-start(f32[40,1,1,1,128,128]{5,4,0,3,2,1:T(8,128)} %fusion.192) | copy-start | bytes 7864324
  648.7 19.3 %copy-start.7 = (f32[40,1,1,1,128,128]{5,4,0,3,2,1:T(8,128)S(1)}, f32[40,1,1,1,128,128]{5,4,0,3,2,1:T(8,128)}, u32[]{:S(2)}) copy-start(f32[40,1,1,1,128,128]{5,4,0,3,2,1:T(8,128)} %fusion.193) | copy-start | bytes 7864324
  648.8 19.3 %copy-start.10 = (f32[40,1,1,3]{0,3,2,1:T(4,128)S(1)}, f32[40,1,1,3]{0,3,2,1:T(4,128)}, u32[]{:S(2)}) copy-start(f32[40,1,1,3]{0,3,2,1:T(4,128)} %copy-done.9) | copy-start | bytes 1444
Sparse Core Ops, SparseCore 0:
  15.3 529.8 all-gather.1
